TPU v7x, 32 devices: a whole 2x2x4 slice. The times are simulated.
32 devices in a mesh: groups: 2 (over y), blk: 4 (over x, core), ulysses: 4 (over z).
Axes of the slice: x: 2, y: 2, z: 4, core: 2. Of those that a mesh axis runs over, the one named last changes fastest.
Arguments:
- query_proj: bfloat16 [1024, 1024], P(('groups', 'blk', 'ulysses')), parts along dimension 0, may hold values from -200 to 200
- key_proj: bfloat16 [1024, 1024], P(('groups', 'blk', 'ulysses')), parts along dimension 0, may hold values from -200 to 200
- value_proj: bfloat16 [1024, 1024], P(('groups', 'blk', 'ulysses')), parts along dimension 0, may hold values from -6 to 6
- query_gain: float32 [1024], replicated, may hold values from 1.2 to 2.4
- key_gain: float32 [1024], replicated, may hold values from 1.2 to 2.4
- control: bfloat16 [1024, 384], P(('groups', 'blk', 'ulysses')), parts along dimension 0, may hold values from -6 to 6
- hint_weight: bfloat16 [384, 1024], replicated, may hold values from -0.3125 to 0.3125
- hint_gain: float32 [8, 1024], replicated, may hold values from 0.3 to 3
- owner_map: int32 [32, 4], P(('groups', 'blk', 'ulysses')), parts along dimension 0, may hold values from 0 to 3, each once within a row
- layer_index: int32 [32], P(('groups', 'blk', 'ulysses')), parts along dimension 0, may hold values from 0 to 7
Outputs:
- block_out: bfloat16 [1024, 1024], P(('groups', 'blk', 'ulysses')), parts along dimension 0
There are 2 independent parts, one for each index of `groups`. A program takes and returns all parts, laid end to end along the dimension named above; an argument that names none is the same for every part. Nothing has to cross between parts.
Inputs may be any that keep to these rules, and one draw needn't show every extreme that they name: `owner_map`: each row is a permutation of 0 to 3.
All inputs are finite; a program needn't handle non-finite values.
Results may differ from a plain program's by a relative error of at most 0.008.
Values may be sent and summed in bfloat16 or wider, within the bound.
A program may use at most 64 MiB of HBM per device.

v0:
```python
import functools
import math

import jax
import jax.numpy as jnp
from jax import lax
from jax.experimental import pallas as pl
from jax.experimental.pallas import tpu as pltpu
from jax.sharding import PartitionSpec as P

HEAD_DIM = 128
CORES = 2
MESH = pl.DeviceIdType.MESH


def normalize_rows(rows, gain):
    values = rows.astype(jnp.float32)
    scale = lax.rsqrt(jnp.mean(values * values, axis=-1, keepdims=True) + 1e-06)
    return (values * scale * gain).astype(jnp.bfloat16)


def block_size(count):
    block = min(count, 1024)
    while count % block:
        block = block - 1
    return block


def make_fold(queries):
    rows = queries.shape[0]
    heads = queries.shape[1] // HEAD_DIM
    shaped = queries.reshape(rows, heads, HEAD_DIM)
    factor = HEAD_DIM ** (-0.5)

    def update(state, pair):
        peak, totals, accum = state
        key_block, value_block = pair
        scores = (
            jnp.einsum("qhd,khd->hqk", shaped, key_block, preferred_element_type=jnp.float32)
            * factor
        )
        new_peak = jnp.maximum(peak, jnp.max(scores, axis=-1))
        correction = jnp.exp(peak - new_peak)
        expo = jnp.exp(scores - new_peak[:, :, None])
        totals = totals * correction + jnp.sum(expo, axis=-1)
        mixed = jnp.einsum(
            "hqk,khd->hqd",
            expo.astype(jnp.bfloat16),
            value_block,
            preferred_element_type=jnp.float32,
        )
        accum = accum * correction[:, :, None] + mixed
        return ((new_peak, totals, accum), None)

    def fold(carry, piece, start):
        keys, values = piece
        count = keys.shape[0]
        block = block_size(count)
        key_blocks = keys.reshape(count // block, block, heads, HEAD_DIM)
        value_blocks = values.reshape(count // block, block, heads, HEAD_DIM)
        result, unused = lax.scan(update, carry, (key_blocks, value_blocks))
        return result

    start_state = (
        jnp.full((heads, rows), -1e30, jnp.float32),
        jnp.zeros((heads, rows), jnp.float32),
        jnp.zeros((heads, rows, HEAD_DIM), jnp.float32),
    )
    return (fold, start_state)


def finish(state):
    peak, totals, accum = state
    heads, rows = totals.shape
    output = (accum / totals[:, :, None]).astype(jnp.bfloat16)
    return output.transpose(1, 0, 2).reshape(rows, heads * HEAD_DIM)


def make_hint(patches, hint_weight):
    normed = normalize_rows(patches, jnp.float32(1.0))
    return jnp.dot(normed, hint_weight, preferred_element_type=jnp.float32).astype(jnp.bfloat16)


def shards(
    query_proj,
    key_proj,
    value_proj,
    query_gain,
    key_gain,
    control,
    hint_weight,
    hint_gain,
    owner_map,
    layer_index,
):
    query_normed = normalize_rows(query_proj, query_gain)
    key_normed = normalize_rows(key_proj, key_gain)
    query_heads, key_heads, value_heads = (
        lax.all_to_all(query_normed, "ulysses", split_axis=1, concat_axis=0, tiled=True),
        lax.all_to_all(key_normed, "ulysses", split_axis=1, concat_axis=0, tiled=True),
        lax.all_to_all(value_proj, "ulysses", split_axis=1, concat_axis=0, tiled=True),
    )
    fold, start_state = make_fold(query_heads)
    state = fold(
        start_state,
        (
            lax.all_gather(key_heads, "blk", axis=0, tiled=True),
            lax.all_gather(value_heads, "blk", axis=0, tiled=True),
        ),
        jnp.int32(0),
    )
    attended = lax.all_to_all(finish(state), "ulysses", split_axis=0, concat_axis=1, tiled=True)
    owners = lax.axis_size("ulysses")
    tok_rows = control.shape[0]
    slab_rows = tok_rows // owners
    positions = jnp.arange(owners, dtype=jnp.int32)
    match = (owner_map[0][:, None] == positions[None, :]).astype(jnp.int32)
    inverse = jnp.sum(positions[:, None] * match, axis=0)
    gain_row = lax.dynamic_index_in_dim(hint_gain, layer_index[0], 0, keepdims=False)
    outgoing = jnp.take(control.reshape(owners, slab_rows, control.shape[1]), inverse, axis=0)
    arrived = lax.all_to_all(outgoing, "ulysses", split_axis=0, concat_axis=0, tiled=True).reshape(
        tok_rows, control.shape[1]
    )
    placed = make_hint(arrived, hint_weight)
    return (attended.astype(jnp.float32) + placed.astype(jnp.float32) * gain_row).astype(
        jnp.bfloat16
    )


def row_scale(values):
    return lax.rsqrt(jnp.mean(values * values, axis=-1, keepdims=True) + 1e-06)


def kernel(
    blks,
    owners,
    query_hbm,
    key_hbm,
    value_hbm,
    query_gain_hbm,
    key_gain_hbm,
    control_hbm,
    weight_hbm,
    gain_hbm,
    owner_hbm,
    layer_smem,
    out_ref,
    query_in,
    key_in,
    value_in,
    query_gain,
    key_gain,
    control_in,
    weight,
    gains,
    owner_smem,
    stage,
    landed,
    slabs_out,
    slabs_in,
    mixed_out,
    attended,
    hint,
    load_sem,
    send_sem,
    recv_sem,
    slab_send,
    slab_recv,
    back_send,
    back_recv,
    level_sem,
):
    rows = query_in.shape[0]
    low, high = host_range(owners)
    wide = high - low
    heads = blks * wide
    cols = blks // CORES
    devices = blks * owners
    slab_rows = rows // owners
    b = lax.axis_index("blk")
    u = lax.axis_index("ulysses")
    parity = lax.rem(b, CORES)
    x = b // CORES
    me = b * owners + u
    own = b * wide + u - low
    hosting = (u >= low) & (u < high)

    loads = [
        pltpu.make_async_copy(source, target, load_sem.at[at])
        for at, (source, target) in enumerate(
            (
                (query_hbm, query_in),
                (query_gain_hbm, query_gain),
                (key_hbm, key_in),
                (key_gain_hbm, key_gain),
                (value_hbm, value_in),
                (control_hbm, control_in),
                (weight_hbm, weight),
                (gain_hbm, gains),
                (owner_hbm, owner_smem),
            )
        )
    ]
    for load in loads:
        load.start()

    around = (
        (b >= 0, {"blk": x * CORES + (1 - parity)}),
        (u > 0, {"ulysses": u - 1}),
        (u < owners - 1, {"ulysses": u + 1}),
        (x > 0, {"blk": b - CORES}),
        (x < cols - 1, {"blk": b + CORES}),
    )
    near = (
        1
        + (u + owners - 1) // owners
        + (2 * owners - 2 - u) // owners
        + (x + cols - 1) // cols
        + (2 * cols - 2 - x) // cols
    )

    def tell(semaphore):
        for inside, device in around:

            @pl.when(inside)
            def _():
                pl.semaphore_signal(
                    semaphore, inc=1, device_id=device, device_id_type=MESH
                )

    def hops(to_b, to_u):
        return (
            jnp.abs(to_b // CORES - x) + jnp.abs(to_b % CORES - parity) + jnp.abs(to_u - u)
        )

    reach = max(max(high - 1, owners - 1 - low) + cols, owners - 1)
    barrier = pltpu.get_barrier_semaphore()
    tell(barrier)
    pl.semaphore_wait(barrier, near)
    tell(level_sem.at[2])

    for first, gain, part in ((query_in, query_gain, 0), (key_in, key_gain, 1)):
        loads[2 * part].wait()
        loads[2 * part + 1].wait()
        values = first[...].astype(jnp.float32)
        normed = (values * row_scale(values) * gain[...]).astype(jnp.bfloat16)
        for h in range(heads):
            stage[h, part * rows : (part + 1) * rows] = normed[
                :, h * HEAD_DIM : (h + 1) * HEAD_DIM
            ]
    loads[4].wait()
    for h in range(heads):
        stage[h, 2 * rows :] = value_in[:, h * HEAD_DIM : (h + 1) * HEAD_DIM]

    started = []

    def remote(source, target, sem_out, sem_in, device):
        return pltpu.make_async_remote_copy(
            src_ref=source,
            dst_ref=target,
            send_sem=sem_out,
            recv_sem=sem_in,
            device_id=device,
            device_id_type=MESH,
        )

    def send(*way):
        copy = remote(*way)
        copy.start()
        started.append(copy)

    def arrive(target, sem_out, sem_in):
        pltpu.make_async_remote_copy(
            src_ref=target,
            dst_ref=target,
            send_sem=sem_out,
            recv_sem=sem_in,
            device_id={"blk": x * CORES + (1 - parity)},
            device_id_type=MESH,
        ).wait_recv()

    hosts = [(h, h // wide, low + h % wide) for h in range(heads)]
    for distance in range(1, reach + 1):
        if distance > 1:
            pl.semaphore_wait(level_sem.at[distance], near)
            if distance < reach:
                tell(level_sem.at[distance + 1])
        for h, to_b, to_u in hosts:

            @pl.when(hops(to_b, to_u) == distance)
            def _():
                remote(
                    stage.at[h],
                    landed.at[me],
                    send_sem.at[h],
                    recv_sem.at[me],
                    {"blk": to_b, "ulysses": to_u},
                ).start()

    loads[5].wait()
    loads[8].wait()
    values = control_in[...].astype(jnp.float32)
    normed = values * row_scale(values)
    pieces = [normed[j * slab_rows : (j + 1) * slab_rows] for j in range(owners)]
    for to in range(owners):
        picked = pieces[0]
        for j in range(1, owners):
            picked = jnp.where(owner_smem[0, j] == to, pieces[j], picked)
        slabs_out[to] = picked.astype(jnp.bfloat16)

    for d in range(1, owners):
        there = lax.rem(u + d, owners)
        send(
            slabs_out.at[there],
            slabs_in.at[u],
            slab_send.at[d],
            slab_recv.at[u],
            {"ulysses": there},
        )
    slabs_in[u] = slabs_out[u]

    order = [
        (to_b, to_u)
        for to_u in sorted(range(owners), key=lambda at: (low <= at < high, at))
        for to_b in range(blks)
    ]
    factor = HEAD_DIM ** (-0.5) * math.log2(math.e)

    @pl.when(hosting)
    def _():
        landed[me] = stage[own]
        for to_b, to_u in order:
            there = to_b * owners + to_u

            @pl.when(there != me)
            def _():
                arrive(landed.at[there], back_send.at[0], recv_sem.at[there])

        count = devices * rows
        keys = landed[:, rows : 2 * rows].reshape(count, HEAD_DIM)
        mix = landed[:, 2 * rows :].reshape(count, HEAD_DIM)
        group = devices // GROUPS

        def flush(base):
            for to_b, to_u in order[base : base + group]:
                there = to_b * owners + to_u

                @pl.when(there != me)
                def _():
                    remote(
                        mixed_out.at[there],
                        attended.at[own],
                        back_send.at[there],
                        back_recv.at[own],
                        {"blk": to_b, "ulysses": to_u},
                    ).start()

        for base in range(0, devices, group):
            part = [to_b * owners + to_u for to_b, to_u in order[base : base + group]]
            queries = jnp.concatenate([landed[there, :rows] for there in part], axis=0)
            scores = lax.dot_general(
                queries, keys, (((1,), (1,)), ((), ())), preferred_element_type=jnp.float32
            )
            peak = jnp.max(scores, axis=-1, keepdims=True)
            expo = jnp.exp2((scores - peak) * factor)
            totals = jnp.sum(expo, axis=-1, keepdims=True)
            output = jnp.dot(
                expo.astype(jnp.bfloat16), mix, preferred_element_type=jnp.float32
            )
            output = (output * (1.0 / totals)).astype(jnp.bfloat16)
            if base:
                flush(base - group)
            for at, there in enumerate(part):
                mixed_out[there] = output[at * rows : (at + 1) * rows]
        flush(devices - group)
        attended[own] = mixed_out[me]

    loads[6].wait()
    loads[7].wait()
    for d in range(1, owners):
        source = lax.rem(u + owners - d, owners)
        arrive(slabs_in.at[source], slab_send.at[0], slab_recv.at[source])
    arrived = slabs_in[...].astype(jnp.float32).reshape(rows, control_in.shape[1])
    placed = jnp.dot(
        arrived.astype(jnp.bfloat16), weight[...], preferred_element_type=jnp.float32
    ).astype(jnp.bfloat16)
    hint[...] = placed.astype(jnp.float32) * gains[pl.ds(layer_smem[0], 1), :]

    for h, to_b, to_u in hosts:

        @pl.when(hops(to_b, to_u) > 0)
        def _():
            arrive(attended.at[h], back_send.at[0], back_recv.at[h])
            remote(
                stage.at[h], landed.at[me], send_sem.at[h], recv_sem.at[me], around[0][1]
            ).wait_send()

    for h in range(heads):
        columns = slice(h * HEAD_DIM, (h + 1) * HEAD_DIM)
        out_ref[:, columns] = (attended[h].astype(jnp.float32) + hint[:, columns]).astype(
            jnp.bfloat16
        )
    for copy in started:
        copy.wait_send()

    @pl.when(hosting)
    def _():
        for there in range(devices):

            @pl.when(there != me)
            def _():
                remote(
                    mixed_out.at[there],
                    attended.at[own],
                    back_send.at[there],
                    back_recv.at[own],
                    around[0][1],
                ).wait_send()


GROUPS = 4


def host_range(owners):
    low = owners // 4
    return (low, owners - low)


def run(blks, owners, *arrays):
    query_proj, control, hint_weight, hint_gain = arrays[0], arrays[5], arrays[6], arrays[7]
    rows, feats = query_proj.shape
    low, high = host_range(owners)
    heads = blks * (high - low)
    devices = blks * owners
    fits = (
        blks % CORES == 0
        and owners > 1
        and heads * HEAD_DIM == feats
        and devices % GROUPS == 0
        and rows % 16 == 0
        and rows % owners == 0
        and (rows // owners) % 8 == 0
        and rows * devices <= 1024
    )
    if not fits:
        return shards(*arrays)
    inner = control.shape[1]
    dma = pltpu.SemaphoreType.DMA
    half = jnp.bfloat16
    wide = jnp.float32
    operands = list(arrays)
    operands[3] = arrays[3].reshape(1, feats)
    operands[4] = arrays[4].reshape(1, feats)
    layer = operands.pop()
    operands = [pltpu.with_memory_space_constraint(array, pltpu.HBM) for array in operands]
    return pl.pallas_call(
        functools.partial(kernel, blks, owners),
        out_shape=jax.ShapeDtypeStruct((rows, feats), half),
        in_specs=[pl.BlockSpec(memory_space=pltpu.HBM)] * len(operands)
        + [pl.BlockSpec(memory_space=pltpu.SMEM)],
        out_specs=pl.BlockSpec(memory_space=pltpu.VMEM),
        scratch_shapes=[
            pltpu.VMEM((rows, feats), half),
            pltpu.VMEM((rows, feats), half),
            pltpu.VMEM((rows, feats), half),
            pltpu.VMEM((1, feats), wide),
            pltpu.VMEM((1, feats), wide),
            pltpu.VMEM((rows, inner), half),
            pltpu.VMEM(hint_weight.shape, half),
            pltpu.VMEM(hint_gain.shape, wide),
            pltpu.SMEM((1, owners), jnp.int32),
            pltpu.VMEM((heads, 3 * rows, HEAD_DIM), half),
            pltpu.VMEM((devices, 3 * rows, HEAD_DIM), half),
            pltpu.VMEM((owners, rows // owners, inner), half),
            pltpu.VMEM((owners, rows // owners, inner), half),
            pltpu.VMEM((devices, rows, HEAD_DIM), half),
            pltpu.VMEM((heads, rows, HEAD_DIM), half),
            pltpu.VMEM((rows, feats), wide),
            dma((len(operands),)),
            dma((heads,)),
            dma((devices,)),
            dma((owners,)),
            dma((owners,)),
            dma((devices,)),
            dma((heads,)),
            pltpu.SemaphoreType.REGULAR((blks // CORES + owners + 1,)),
        ],
        compiler_params=pltpu.CompilerParams(
            collective_id=0, has_side_effects=True, vmem_limit_bytes=16 << 20
        ),
    )(*operands, layer)


def solution(mesh):
    return jax.shard_map(
        functools.partial(run, mesh.shape["blk"], mesh.shape["ulysses"]),
        mesh=mesh,
        in_specs=(
            P(("groups", "blk", "ulysses"), None),
            P(("groups", "blk", "ulysses"), None),
            P(("groups", "blk", "ulysses"), None),
            P(),
            P(),
            P(("groups", "blk", "ulysses"), None),
            P(),
            P(),
            P(("groups", "blk", "ulysses"), None),
            P(("groups", "blk", "ulysses")),
        ),
        out_specs=P(("groups", "blk", "ulysses"), None),
        check_vma=False,
    )
```

profile of v0, /device:TPU:0, one launch (start us, length us, event | category | flops | bytes accessed | tf_op | source)
XLA Modules:
  0.0 17.6 jit_solution(4159481126746549707)
XLA Ops:
  0.7 16.3 %shard_map.100 = bf16[32,1024]{1,0:T(8,128)(2,1)S(1)} custom-call(bf16[32,1024]{1,0:T(8,128)(2,1)} %query_hbm.1, bf16[32,1024]{1,0:T(8,128)(2,1)} %key_hbm.1, bf16[32,1024]{1,0:T(8,128)(2,1)} %value_hbm.1, f32[1,1024]{1,0:T(1,128)} %bitcast.2, f32[1,1024]{1,0:T(1,128)} %bitcast.3, bf16[32,384]{1,0:T(8,128)(2,1)} %control_hbm.1, ...), custom_call_target="tpu_custom_call" | custom-call | tf_op jit(solution)/shard_map/pallas_call | solution.py:456
  17.0 0.6 %copy.13 = bf16[32,1024]{1,0:T(8,128)(2,1)} copy(bf16[32,1024]{1,0:T(8,128)(2,1)S(1)} %shard_map.100) | data formatting | bytes 131072
where the time goes:
time: 17.7 us; the launch traced here: 17.6 us
  Pallas kernels  16.3 us (92%)
  between operations  0.66 us (4%)
  local copies, waits for them, and re-layouts  0.63 us (4%)
    pallas_call x1, Pallas kernels, run(): pl.pallas_call(functools.partial(kernel, blks, owners), out_shape=jax.Sha...  16.3 us
    unnamed x1, local copies, waits for them, and re-layouts  0.63 us

commit v1 on v0

--- a/solution.py
+++ b/solution.py
@@ -147,7 +147,6 @@
     out_ref,
     query_in,
     key_in,
-    value_in,
     query_gain,
     key_gain,
     control_in,
@@ -162,13 +161,15 @@
     attended,
     hint,
     load_sem,
+    value_sem,
     send_sem,
     recv_sem,
     slab_send,
     slab_recv,
     back_send,
     back_recv,
-    level_sem,
+    far_sem,
+    line_sem,
 ):
     rows = query_in.shape[0]
     low, high = host_range(owners)
@@ -179,11 +180,32 @@
     slab_rows = rows // owners
     b = lax.axis_index("blk")
     u = lax.axis_index("ulysses")
-    parity = lax.rem(b, CORES)
     x = b // CORES
     me = b * owners + u
     own = b * wide + u - low
     hosting = (u >= low) & (u < high)
+    visiting = jnp.logical_not(hosting)
+    near_low = 2 * u < owners
+    near = jnp.where(near_low, low, high - 1)
+    far = jnp.where(near_low, high - 1, low)
+    edge = jnp.where(near_low, 0, owners - 1)
+    partner = {"blk": x * CORES + (1 - lax.rem(b, CORES))}
+
+    def signal(semaphore, device):
+        pl.semaphore_signal(semaphore, inc=1, device_id=device, device_id_type=MESH)
+
+    barrier = pltpu.get_barrier_semaphore()
+    for to_b in range(blks):
+        signal(barrier, {"blk": to_b, "ulysses": jnp.where(hosting, far, near)})
+
+    @pl.when(hosting)
+    def _():
+        for to_b in range(blks):
+            signal(barrier, {"blk": to_b, "ulysses": edge})
+
+            @pl.when(to_b != b)
+            def _():
+                signal(barrier, {"blk": to_b})
 
     loads = [
         pltpu.make_async_copy(source, target, load_sem.at[at])
@@ -193,66 +215,15 @@
                 (query_gain_hbm, query_gain),
                 (key_hbm, key_in),
                 (key_gain_hbm, key_gain),
-                (value_hbm, value_in),
                 (control_hbm, control_in),
+                (owner_hbm, owner_smem),
                 (weight_hbm, weight),
                 (gain_hbm, gains),
-                (owner_hbm, owner_smem),
             )
         )
     ]
     for load in loads:
         load.start()
-
-    around = (
-        (b >= 0, {"blk": x * CORES + (1 - parity)}),
-        (u > 0, {"ulysses": u - 1}),
-        (u < owners - 1, {"ulysses": u + 1}),
-        (x > 0, {"blk": b - CORES}),
-        (x < cols - 1, {"blk": b + CORES}),
-    )
-    near = (
-        1
-        + (u + owners - 1) // owners
-        + (2 * owners - 2 - u) // owners
-        + (x + cols - 1) // cols
-        + (2 * cols - 2 - x) // cols
-    )
-
-    def tell(semaphore):
-        for inside, device in around:
-
-            @pl.when(inside)
-            def _():
-                pl.semaphore_signal(
-                    semaphore, inc=1, device_id=device, device_id_type=MESH
-                )
-
-    def hops(to_b, to_u):
-        return (
-            jnp.abs(to_b // CORES - x) + jnp.abs(to_b % CORES - parity) + jnp.abs(to_u - u)
-        )
-
-    reach = max(max(high - 1, owners - 1 - low) + cols, owners - 1)
-    barrier = pltpu.get_barrier_semaphore()
-    tell(barrier)
-    pl.semaphore_wait(barrier, near)
-    tell(level_sem.at[2])
-
-    for first, gain, part in ((query_in, query_gain, 0), (key_in, key_gain, 1)):
-        loads[2 * part].wait()
-        loads[2 * part + 1].wait()
-        values = first[...].astype(jnp.float32)
-        normed = (values * row_scale(values) * gain[...]).astype(jnp.bfloat16)
-        for h in range(heads):
-            stage[h, part * rows : (part + 1) * rows] = normed[
-                :, h * HEAD_DIM : (h + 1) * HEAD_DIM
-            ]
-    loads[4].wait()
-    for h in range(heads):
-        stage[h, 2 * rows :] = value_in[:, h * HEAD_DIM : (h + 1) * HEAD_DIM]
-
-    started = []
 
     def remote(source, target, sem_out, sem_in, device):
         return pltpu.make_async_remote_copy(
@@ -264,41 +235,74 @@
             device_id_type=MESH,
         )
 
-    def send(*way):
-        copy = remote(*way)
-        copy.start()
-        started.append(copy)
-
-    def arrive(target, sem_out, sem_in):
-        pltpu.make_async_remote_copy(
-            src_ref=target,
-            dst_ref=target,
-            send_sem=sem_out,
-            recv_sem=sem_in,
-            device_id={"blk": x * CORES + (1 - parity)},
-            device_id_type=MESH,
-        ).wait_recv()
-
-    hosts = [(h, h // wide, low + h % wide) for h in range(heads)]
-    for distance in range(1, reach + 1):
-        if distance > 1:
-            pl.semaphore_wait(level_sem.at[distance], near)
-            if distance < reach:
-                tell(level_sem.at[distance + 1])
-        for h, to_b, to_u in hosts:
-
-            @pl.when(hops(to_b, to_u) == distance)
+    def drain(target, semaphore):
+        pltpu.make_async_copy(target, target, semaphore).wait()
+
+    values_at, normed_at = pl.ds(2 * rows, rows), pl.ds(0, 2 * rows)
+
+    def columns_of(h):
+        return pl.ds(pl.multiple_of(h * HEAD_DIM, HEAD_DIM), HEAD_DIM)
+
+    def send(source, span, core, to_u):
+        for aside in (*range(1, cols), 0):
+            to_b = lax.rem(x + aside, cols) * CORES + core
+
+            @pl.when((to_b != b) | (to_u != u))
             def _():
+                h = to_b * wide + to_u - low
                 remote(
-                    stage.at[h],
-                    landed.at[me],
-                    send_sem.at[h],
-                    recv_sem.at[me],
+                    source(h),
+                    landed.at[me, span],
+                    send_sem,
+                    recv_sem,
                     {"blk": to_b, "ulysses": to_u},
                 ).start()
 
+    def send_values(to_u):
+        for core in range(CORES):
+            send(lambda h: value_hbm.at[:, columns_of(h)], values_at, core, to_u)
+
+    own_values = pltpu.make_async_copy(
+        value_hbm.at[:, columns_of(jnp.where(hosting, own, 0))],
+        landed.at[me, values_at],
+        value_sem,
+    )
+
+    @pl.when(hosting)
+    def _():
+        own_values.start()
+        pl.semaphore_wait(barrier, 3 * blks - 1)
+        signal(far_sem, {"ulysses": edge})
+        signal(far_sem, {"ulysses": far})
+        send_values(far)
+        send_values(near)
+
+    @pl.when(visiting)
+    def _():
+        pl.semaphore_wait(barrier, blks)
+        send_values(near)
+
+    for load in loads[:4]:
+        load.wait()
+    for first, gain, part in ((query_in, query_gain, 0), (key_in, key_gain, 1)):
+        values = first[...].astype(jnp.float32)
+        normed = (values * row_scale(values) * gain[...]).astype(jnp.bfloat16)
+        for h in range(heads):
+            stage[h, part * rows : (part + 1) * rows] = normed[
+                :, h * HEAD_DIM : (h + 1) * HEAD_DIM
+            ]
+
+    @pl.when(visiting)
+    def _():
+        pl.semaphore_wait(far_sem, 1)
+        send_values(far)
+
+    for core in range(CORES):
+        for to_u in (far, near):
+            send(lambda h: stage.at[h], normed_at, core, to_u)
+
+    loads[4].wait()
     loads[5].wait()
-    loads[8].wait()
     values = control_in[...].astype(jnp.float32)
     normed = values * row_scale(values)
     pieces = [normed[j * slab_rows : (j + 1) * slab_rows] for j in range(owners)]
@@ -308,15 +312,20 @@
             picked = jnp.where(owner_smem[0, j] == to, pieces[j], picked)
         slabs_out[to] = picked.astype(jnp.bfloat16)
 
+    @pl.when(hosting)
+    def _():
+        pl.semaphore_wait(far_sem, 1)
+        signal(line_sem, {"ulysses": edge})
+
+    @pl.when(visiting)
+    def _():
+        pl.semaphore_wait(line_sem, 1)
+
     for d in range(1, owners):
         there = lax.rem(u + d, owners)
-        send(
-            slabs_out.at[there],
-            slabs_in.at[u],
-            slab_send.at[d],
-            slab_recv.at[u],
-            {"ulysses": there},
-        )
+        remote(
+            slabs_out.at[there], slabs_in.at[u], slab_send, slab_recv, {"ulysses": there}
+        ).start()
     slabs_in[u] = slabs_out[u]
 
     order = [
@@ -328,13 +337,9 @@
 
     @pl.when(hosting)
     def _():
-        landed[me] = stage[own]
-        for to_b, to_u in order:
-            there = to_b * owners + to_u
-
-            @pl.when(there != me)
-            def _():
-                arrive(landed.at[there], back_send.at[0], recv_sem.at[there])
+        landed[me, normed_at] = stage[own]
+        own_values.wait()
+        drain(landed.at[pl.ds(0, devices - 1)], recv_sem)
 
         count = devices * rows
         keys = landed[:, rows : 2 * rows].reshape(count, HEAD_DIM)
@@ -350,8 +355,8 @@
                     remote(
                         mixed_out.at[there],
                         attended.at[own],
-                        back_send.at[there],
-                        back_recv.at[own],
+                        back_send,
+                        back_recv,
                         {"blk": to_b, "ulysses": to_u},
                     ).start()
 
@@ -368,54 +373,37 @@
                 expo.astype(jnp.bfloat16), mix, preferred_element_type=jnp.float32
             )
             output = (output * (1.0 / totals)).astype(jnp.bfloat16)
-            if base:
-                flush(base - group)
             for at, there in enumerate(part):
                 mixed_out[there] = output[at * rows : (at + 1) * rows]
-        flush(devices - group)
+            flush(base)
         attended[own] = mixed_out[me]
 
     loads[6].wait()
     loads[7].wait()
-    for d in range(1, owners):
-        source = lax.rem(u + owners - d, owners)
-        arrive(slabs_in.at[source], slab_send.at[0], slab_recv.at[source])
+    drain(slabs_in.at[pl.ds(0, owners - 1)], slab_recv)
     arrived = slabs_in[...].astype(jnp.float32).reshape(rows, control_in.shape[1])
     placed = jnp.dot(
         arrived.astype(jnp.bfloat16), weight[...], preferred_element_type=jnp.float32
     ).astype(jnp.bfloat16)
     hint[...] = placed.astype(jnp.float32) * gains[pl.ds(layer_smem[0], 1), :]
-
-    for h, to_b, to_u in hosts:
-
-        @pl.when(hops(to_b, to_u) > 0)
-        def _():
-            arrive(attended.at[h], back_send.at[0], back_recv.at[h])
-            remote(
-                stage.at[h], landed.at[me], send_sem.at[h], recv_sem.at[me], around[0][1]
-            ).wait_send()
+    drain(slabs_in.at[pl.ds(0, owners - 1)], slab_send)
+
+    @pl.when(hosting)
+    def _():
+        drain(landed.at[pl.ds(0, heads - 1)], send_sem)
+        drain(mixed_out.at[pl.ds(0, devices - 1)], back_send)
+        drain(attended.at[pl.ds(0, heads - 1)], back_recv)
+
+    @pl.when(visiting)
+    def _():
+        drain(landed.at[pl.ds(0, heads)], send_sem)
+        drain(attended, back_recv)
 
     for h in range(heads):
         columns = slice(h * HEAD_DIM, (h + 1) * HEAD_DIM)
         out_ref[:, columns] = (attended[h].astype(jnp.float32) + hint[:, columns]).astype(
             jnp.bfloat16
         )
-    for copy in started:
-        copy.wait_send()
-
-    @pl.when(hosting)
-    def _():
-        for there in range(devices):
-
-            @pl.when(there != me)
-            def _():
-                remote(
-                    mixed_out.at[there],
-                    attended.at[own],
-                    back_send.at[there],
-                    back_recv.at[own],
-                    around[0][1],
-                ).wait_send()
 
 
 GROUPS = 4
@@ -436,6 +424,8 @@
         blks % CORES == 0
         and owners > 1
         and heads * HEAD_DIM == feats
+        and (low, high) == (1, owners - 1)
+        and high - low == 2
         and devices % GROUPS == 0
         and rows % 16 == 0
         and rows % owners == 0
@@ -462,14 +452,13 @@
         scratch_shapes=[
             pltpu.VMEM((rows, feats), half),
             pltpu.VMEM((rows, feats), half),
-            pltpu.VMEM((rows, feats), half),
             pltpu.VMEM((1, feats), wide),
             pltpu.VMEM((1, feats), wide),
             pltpu.VMEM((rows, inner), half),
             pltpu.VMEM(hint_weight.shape, half),
             pltpu.VMEM(hint_gain.shape, wide),
             pltpu.SMEM((1, owners), jnp.int32),
-            pltpu.VMEM((heads, 3 * rows, HEAD_DIM), half),
+            pltpu.VMEM((heads, 2 * rows, HEAD_DIM), half),
             pltpu.VMEM((devices, 3 * rows, HEAD_DIM), half),
             pltpu.VMEM((owners, rows // owners, inner), half),
             pltpu.VMEM((owners, rows // owners, inner), half),
@@ -477,13 +466,15 @@
             pltpu.VMEM((heads, rows, HEAD_DIM), half),
             pltpu.VMEM((rows, feats), wide),
             dma((len(operands),)),
-            dma((heads,)),
-            dma((devices,)),
-            dma((owners,)),
-            dma((owners,)),
-            dma((devices,)),
-            dma((heads,)),
-            pltpu.SemaphoreType.REGULAR((blks // CORES + owners + 1,)),
+            dma,
+            dma,
+            dma,
+            dma,
+            dma,
+            dma,
+            dma,
+            pltpu.SemaphoreType.REGULAR,
+            pltpu.SemaphoreType.REGULAR,
         ],
         compiler_params=pltpu.CompilerParams(
             collective_id=0, has_side_effects=True, vmem_limit_bytes=16 << 20

time: 17.7 us -> 16.9 us (0.955)
  Pallas kernels: 16.3 us -> 15.5 us
    pallas_call x1, Pallas kernels: 16.3 us -> 15.5 us  [run(): pl.pallas_call(functools.partial(kernel, blks, owners), out_shape=jax.Sha...]
where the time goes in v1:
time: 16.9 us; the launch traced here: 16.8 us
  Pallas kernels  15.5 us (92%)
  between operations  0.66 us (4%)
  local copies, waits for them, and re-layouts  0.63 us (4%)
    pallas_call x1, Pallas kernels, run(): pl.pallas_call(functools.partial(kernel, blks, owners), out_shape=jax.Sha...  15.5 us
    unnamed x1, local copies, waits for them, and re-layouts  0.63 us

profile of v1, /device:TPU:0, one launch (start us, length us, event | category | flops | bytes accessed | tf_op | source)
XLA Modules:
  0.0 16.8 jit_solution(15477571235449420850)
XLA Ops:
  0.7 15.5 %shard_map.100 = bf16[32,1024]{1,0:T(8,128)(2,1)S(1)} custom-call(bf16[32,1024]{1,0:T(8,128)(2,1)} %query_hbm.1, bf16[32,1024]{1,0:T(8,128)(2,1)} %key_hbm.1, bf16[32,1024]{1,0:T(8,128)(2,1)} %value_hbm.1, f32[1,1024]{1,0:T(1,128)} %bitcast.2, f32[1,1024]{1,0:T(1,128)} %bitcast.3, bf16[32,384]{1,0:T(8,128)(2,1)} %control_hbm.1, ...), custom_call_target="tpu_custom_call" | custom-call | tf_op jit(solution)/shard_map/pallas_call | solution.py:446
  16.2 0.6 %copy.13 = bf16[32,1024]{1,0:T(8,128)(2,1)} copy(bf16[32,1024]{1,0:T(8,128)(2,1)S(1)} %shard_map.100) | data formatting | bytes 131072

commit v2 on v1

--- a/solution.py
+++ b/solution.py
@@ -185,27 +185,33 @@
     own = b * wide + u - low
     hosting = (u >= low) & (u < high)
     visiting = jnp.logical_not(hosting)
+    first_plane = u == 0
+    last_plane = u == owners - 1
+    leading = u == low
     near_low = 2 * u < owners
     near = jnp.where(near_low, low, high - 1)
     far = jnp.where(near_low, high - 1, low)
-    edge = jnp.where(near_low, 0, owners - 1)
     partner = {"blk": x * CORES + (1 - lax.rem(b, CORES))}
 
     def signal(semaphore, device):
         pl.semaphore_signal(semaphore, inc=1, device_id=device, device_id_type=MESH)
 
     barrier = pltpu.get_barrier_semaphore()
-    for to_b in range(blks):
-        signal(barrier, {"blk": to_b, "ulysses": jnp.where(hosting, far, near)})
-
     @pl.when(hosting)
     def _():
-        for to_b in range(blks):
-            signal(barrier, {"blk": to_b, "ulysses": edge})
-
-            @pl.when(to_b != b)
-            def _():
-                signal(barrier, {"blk": to_b})
+        for to_u in range(owners - 1, -1, -1):
+            for to_b in range(blks):
+                told = (to_b != b) | (u != to_u)
+                if to_u == 0:
+                    told = leading
+
+                @pl.when(told)
+                def _():
+                    signal(barrier, {"blk": to_b, "ulysses": to_u})
+
+    @pl.when(first_plane)
+    def _():
+        signal(barrier, {"ulysses": low})
 
     loads = [
         pltpu.make_async_copy(source, target, load_sem.at[at])
@@ -271,15 +277,27 @@
     @pl.when(hosting)
     def _():
         own_values.start()
-        pl.semaphore_wait(barrier, 3 * blks - 1)
-        signal(far_sem, {"ulysses": edge})
-        signal(far_sem, {"ulysses": far})
+
+    @pl.when(first_plane)
+    def _():
+        pl.semaphore_wait(barrier, blks)
+        send_values(near)
+
+    @pl.when(jnp.logical_not(first_plane))
+    def _():
+        pl.semaphore_wait(barrier, heads - hosting.astype(jnp.int32) + leading.astype(jnp.int32))
+
+        @pl.when(leading)
+        def _():
+            signal(far_sem, {"ulysses": 0})
+            signal(line_sem, {"ulysses": far})
+
+        @pl.when(last_plane)
+        def _():
+            for to_u in range(low, high):
+                signal(far_sem, {"ulysses": to_u})
+
         send_values(far)
-        send_values(near)
-
-    @pl.when(visiting)
-    def _():
-        pl.semaphore_wait(barrier, blks)
         send_values(near)
 
     for load in loads[:4]:
@@ -292,14 +310,24 @@
                 :, h * HEAD_DIM : (h + 1) * HEAD_DIM
             ]
 
-    @pl.when(visiting)
-    def _():
+    def send_normed(core, to_u):
+        send(lambda h: stage.at[h], normed_at, core, to_u)
+
+    @pl.when(first_plane)
+    def _():
+        send_normed(0, near)
         pl.semaphore_wait(far_sem, 1)
         send_values(far)
-
-    for core in range(CORES):
-        for to_u in (far, near):
-            send(lambda h: stage.at[h], normed_at, core, to_u)
+        send_normed(0, far)
+
+    @pl.when(jnp.logical_not(first_plane))
+    def _():
+        send_normed(0, far)
+        send_normed(0, near)
+
+    for core in range(1, CORES):
+        send_normed(core, far)
+        send_normed(core, near)
 
     loads[4].wait()
     loads[5].wait()
@@ -315,9 +343,13 @@
     @pl.when(hosting)
     def _():
         pl.semaphore_wait(far_sem, 1)
-        signal(line_sem, {"ulysses": edge})
-
-    @pl.when(visiting)
+
+    @pl.when(leading)
+    def _():
+        for to_u in (0, owners - 1):
+            signal(line_sem, {"ulysses": to_u})
+
+    @pl.when(jnp.logical_not(leading))
     def _():
         pl.semaphore_wait(line_sem, 1)
 

time: 16.9 us -> 16.4 us (0.970)
  Pallas kernels: 15.5 us -> 15 us
    pallas_call x1, Pallas kernels: 15.5 us -> 15 us  [run(): pl.pallas_call(functools.partial(kernel, blks, owners), out_shape=jax.Sha...]
where the time goes in v2:
time: 16.4 us; the launch traced here: 16.3 us
  Pallas kernels  15 us (91%)
  between operations  0.66 us (4%)
  local copies, waits for them, and re-layouts  0.63 us (4%)
    pallas_call x1, Pallas kernels, run(): pl.pallas_call(functools.partial(kernel, blks, owners), out_shape=jax.Sha...  15 us
    unnamed x1, local copies, waits for them, and re-layouts  0.63 us

profile of v2, /device:TPU:0, one launch (start us, length us, event | category | flops | bytes accessed | tf_op | source)
XLA Modules:
  0.0 16.3 jit_solution(11119444000055792467)
XLA Ops:
  0.7 15.0 %shard_map.100 = bf16[32,1024]{1,0:T(8,128)(2,1)S(1)} custom-call(bf16[32,1024]{1,0:T(8,128)(2,1)} %query_hbm.1, bf16[32,1024]{1,0:T(8,128)(2,1)} %key_hbm.1, bf16[32,1024]{1,0:T(8,128)(2,1)} %value_hbm.1, f32[1,1024]{1,0:T(1,128)} %bitcast.2, f32[1,1024]{1,0:T(1,128)} %bitcast.3, bf16[32,384]{1,0:T(8,128)(2,1)} %control_hbm.1, ...), custom_call_target="tpu_custom_call" | custom-call | tf_op jit(solution)/shard_map/pallas_call | solution.py:478
  15.7 0.6 %copy.13 = bf16[32,1024]{1,0:T(8,128)(2,1)} copy(bf16[32,1024]{1,0:T(8,128)(2,1)S(1)} %shard_map.100) | data formatting | bytes 131072

commit v3 on v2

--- a/solution.py
+++ b/solution.py
@@ -164,6 +164,7 @@
     value_sem,
     send_sem,
     recv_sem,
+    query_sem,
     slab_send,
     slab_recv,
     back_send,
@@ -244,12 +245,13 @@
     def drain(target, semaphore):
         pltpu.make_async_copy(target, target, semaphore).wait()
 
-    values_at, normed_at = pl.ds(2 * rows, rows), pl.ds(0, 2 * rows)
+    queries_at, keys_at, values_at = (pl.ds(at * rows, rows) for at in range(3))
+    early = jnp.where(first_plane, 0, 1)
 
     def columns_of(h):
         return pl.ds(pl.multiple_of(h * HEAD_DIM, HEAD_DIM), HEAD_DIM)
 
-    def send(source, span, core, to_u):
+    def send(source, span, semaphore, core, to_u):
         for aside in (*range(1, cols), 0):
             to_b = lax.rem(x + aside, cols) * CORES + core
 
@@ -260,13 +262,12 @@
                     source(h),
                     landed.at[me, span],
                     send_sem,
-                    recv_sem,
+                    semaphore,
                     {"blk": to_b, "ulysses": to_u},
                 ).start()
 
-    def send_values(to_u):
-        for core in range(CORES):
-            send(lambda h: value_hbm.at[:, columns_of(h)], values_at, core, to_u)
+    def send_values(core, to_u):
+        send(lambda h: value_hbm.at[:, columns_of(h)], values_at, recv_sem, core, to_u)
 
     own_values = pltpu.make_async_copy(
         value_hbm.at[:, columns_of(jnp.where(hosting, own, 0))],
@@ -281,7 +282,7 @@
     @pl.when(first_plane)
     def _():
         pl.semaphore_wait(barrier, blks)
-        send_values(near)
+        send_values(0, near)
 
     @pl.when(jnp.logical_not(first_plane))
     def _():
@@ -297,8 +298,9 @@
             for to_u in range(low, high):
                 signal(far_sem, {"ulysses": to_u})
 
-        send_values(far)
-        send_values(near)
+        for to_u in (far, near):
+            for core in range(CORES):
+                send_values(core, to_u)
 
     for load in loads[:4]:
         load.wait()
@@ -310,24 +312,32 @@
                 :, h * HEAD_DIM : (h + 1) * HEAD_DIM
             ]
 
-    def send_normed(core, to_u):
-        send(lambda h: stage.at[h], normed_at, core, to_u)
+    def send_keys(core, to_u):
+        send(lambda h: stage.at[h, keys_at], keys_at, recv_sem, core, to_u)
+
+    def send_queries(core, to_u):
+        send(lambda h: stage.at[h, queries_at], queries_at, query_sem.at[early], core, to_u)
 
     @pl.when(first_plane)
     def _():
-        send_normed(0, near)
+        send_keys(0, near)
+        send_queries(0, near)
+        send_values(1, near)
         pl.semaphore_wait(far_sem, 1)
-        send_values(far)
-        send_normed(0, far)
+        for core in range(CORES):
+            send_values(core, far)
+            send_keys(core, far)
+            send_queries(core, far)
+        for core in range(1, CORES):
+            send_keys(core, near)
+            send_queries(core, near)
 
     @pl.when(jnp.logical_not(first_plane))
     def _():
-        send_normed(0, far)
-        send_normed(0, near)
-
-    for core in range(1, CORES):
-        send_normed(core, far)
-        send_normed(core, near)
+        for part in (send_keys, send_queries):
+            for core in range(CORES):
+                part(core, far)
+                part(core, near)
 
     loads[4].wait()
     loads[5].wait()
@@ -369,14 +379,15 @@
 
     @pl.when(hosting)
     def _():
-        landed[me, normed_at] = stage[own]
+        landed[me, 0 : 2 * rows] = stage[own]
         own_values.wait()
-        drain(landed.at[pl.ds(0, devices - 1)], recv_sem)
+        drain(landed.at[pl.ds(0, devices - 1), pl.ds(0, 2 * rows)], recv_sem)
+        drain(landed.at[pl.ds(0, blks), queries_at], query_sem.at[0])
 
         count = devices * rows
         keys = landed[:, rows : 2 * rows].reshape(count, HEAD_DIM)
         mix = landed[:, 2 * rows :].reshape(count, HEAD_DIM)
-        group = devices // GROUPS
+        group = blks
 
         def flush(base):
             for to_b, to_u in order[base : base + group]:
@@ -393,6 +404,8 @@
                     ).start()
 
         for base in range(0, devices, group):
+            if base == group:
+                drain(landed.at[pl.ds(0, devices - blks - 1), queries_at], query_sem.at[1])
             part = [to_b * owners + to_u for to_b, to_u in order[base : base + group]]
             queries = jnp.concatenate([landed[there, :rows] for there in part], axis=0)
             scores = lax.dot_general(
@@ -438,9 +451,6 @@
         )
 
 
-GROUPS = 4
-
-
 def host_range(owners):
     low = owners // 4
     return (low, owners - low)
@@ -458,7 +468,6 @@
         and heads * HEAD_DIM == feats
         and (low, high) == (1, owners - 1)
         and high - low == 2
-        and devices % GROUPS == 0
         and rows % 16 == 0
         and rows % owners == 0
         and (rows // owners) % 8 == 0
@@ -501,6 +510,7 @@
             dma,
             dma,
             dma,
+            dma((2,)),
             dma,
             dma,
             dma,

time: 16.4 us -> 16.2 us (0.988)
  Pallas kernels: 15 us -> 14.8 us
    pallas_call x1, Pallas kernels: 15 us -> 14.8 us  [run(): pl.pallas_call(functools.partial(kernel, blks, owners), out_shape=jax.Sha...]
where the time goes in v3:
time: 16.2 us; the launch traced here: 16 us
  Pallas kernels  14.8 us (91%)
  between operations  0.66 us (4%)
  local copies, waits for them, and re-layouts  0.63 us (4%)
    pallas_call x1, Pallas kernels, run(): pl.pallas_call(functools.partial(kernel, blks, owners), out_shape=jax.Sha...  14.8 us
    unnamed x1, local copies, waits for them, and re-layouts  0.63 us

profile of v3, /device:TPU:0, one launch (start us, length us, event | category | flops | bytes accessed | tf_op | source)
XLA Modules:
  0.0 16.0 jit_solution(3860487766508696415)
XLA Ops:
  0.7 14.8 %shard_map.100 = bf16[32,1024]{1,0:T(8,128)(2,1)S(1)} custom-call(bf16[32,1024]{1,0:T(8,128)(2,1)} %query_hbm.1, bf16[32,1024]{1,0:T(8,128)(2,1)} %key_hbm.1, bf16[32,1024]{1,0:T(8,128)(2,1)} %value_hbm.1, f32[1,1024]{1,0:T(1,128)} %bitcast.2, f32[1,1024]{1,0:T(1,128)} %bitcast.3, bf16[32,384]{1,0:T(8,128)(2,1)} %control_hbm.1, ...), custom_call_target="tpu_custom_call" | custom-call | tf_op jit(solution)/shard_map/pallas_call | solution.py:487
  15.4 0.6 %copy.13 = bf16[32,1024]{1,0:T(8,128)(2,1)} copy(bf16[32,1024]{1,0:T(8,128)(2,1)S(1)} %shard_map.100) | data formatting | bytes 131072

commit v4 on v3

--- a/solution.py
+++ b/solution.py
@@ -200,15 +200,18 @@
     barrier = pltpu.get_barrier_semaphore()
     @pl.when(hosting)
     def _():
-        for to_u in range(owners - 1, -1, -1):
+        for to_b in range(blks):
+            signal(barrier, {"blk": to_b, "ulysses": far})
+
+        @pl.when(leading)
+        def _():
             for to_b in range(blks):
-                told = (to_b != b) | (u != to_u)
-                if to_u == 0:
-                    told = leading
-
-                @pl.when(told)
-                def _():
-                    signal(barrier, {"blk": to_b, "ulysses": to_u})
+                signal(barrier, {"blk": to_b, "ulysses": 0})
+
+        for to_b in range(blks):
+            signal(barrier, {"blk": to_b, "ulysses": owners - 1})
+        for step in range(1, blks):
+            signal(barrier, {"blk": lax.rem(b + step, blks)})
 
     @pl.when(first_plane)
     def _():
@@ -251,9 +254,9 @@
     def columns_of(h):
         return pl.ds(pl.multiple_of(h * HEAD_DIM, HEAD_DIM), HEAD_DIM)
 
-    def send(source, span, semaphore, core, to_u):
-        for aside in (*range(1, cols), 0):
-            to_b = lax.rem(x + aside, cols) * CORES + core
+    def send(source, span, semaphore, core, to_u, columns=None):
+        for to_x in range(cols - 1, -1, -1) if columns is None else columns:
+            to_b = to_x * CORES + core
 
             @pl.when((to_b != b) | (to_u != u))
             def _():
@@ -266,8 +269,8 @@
                     {"blk": to_b, "ulysses": to_u},
                 ).start()
 
-    def send_values(core, to_u):
-        send(lambda h: value_hbm.at[:, columns_of(h)], values_at, recv_sem, core, to_u)
+    def send_values(core, to_u, *asides):
+        send(lambda h: value_hbm.at[:, columns_of(h)], values_at, recv_sem, core, to_u, *asides)
 
     own_values = pltpu.make_async_copy(
         value_hbm.at[:, columns_of(jnp.where(hosting, own, 0))],
@@ -282,7 +285,8 @@
     @pl.when(first_plane)
     def _():
         pl.semaphore_wait(barrier, blks)
-        send_values(0, near)
+        send_values(0, near, (cols - 1,))
+        send_values(1, near, (cols - 1,))
 
     @pl.when(jnp.logical_not(first_plane))
     def _():
@@ -312,25 +316,33 @@
                 :, h * HEAD_DIM : (h + 1) * HEAD_DIM
             ]
 
-    def send_keys(core, to_u):
-        send(lambda h: stage.at[h, keys_at], keys_at, recv_sem, core, to_u)
-
-    def send_queries(core, to_u):
-        send(lambda h: stage.at[h, queries_at], queries_at, query_sem.at[early], core, to_u)
+    def send_keys(core, to_u, *asides):
+        send(lambda h: stage.at[h, keys_at], keys_at, recv_sem, core, to_u, *asides)
+
+    def send_queries(core, to_u, *asides):
+        send(lambda h: stage.at[h, queries_at], queries_at, query_sem.at[early], core, to_u, *asides)
 
     @pl.when(first_plane)
     def _():
-        send_keys(0, near)
-        send_queries(0, near)
-        send_values(1, near)
+        def bundle(core, to_u, to_x):
+            send_values(core, to_u, (to_x,))
+            send_keys(core, to_u, (to_x,))
+            send_queries(core, to_u, (to_x,))
+
+        def normed_pair(core, to_u, to_x):
+            send_keys(core, to_u, (to_x,))
+            send_queries(core, to_u, (to_x,))
+
+        last = cols - 1
+        normed_pair(0, near, last)
+        normed_pair(1, near, last)
         pl.semaphore_wait(far_sem, 1)
-        for core in range(CORES):
-            send_values(core, far)
-            send_keys(core, far)
-            send_queries(core, far)
-        for core in range(1, CORES):
-            send_keys(core, near)
-            send_queries(core, near)
+        bundle(0, far, last)
+        bundle(1, far, last)
+        bundle(0, far, 0)
+        bundle(0, near, 0)
+        bundle(1, far, 0)
+        bundle(1, near, 0)
 
     @pl.when(jnp.logical_not(first_plane))
     def _():

time: 16.2 us -> 15.8 us (0.975)
  Pallas kernels: 14.8 us -> 14.4 us
    pallas_call x1, Pallas kernels: 14.8 us -> 14.4 us  [run(): pl.pallas_call(functools.partial(kernel, blks, owners), out_shape=jax.Sha...]
where the time goes in v4:
time: 15.8 us; the launch traced here: 15.7 us
  Pallas kernels  14.4 us (91%)
  between operations  0.66 us (4%)
  local copies, waits for them, and re-layouts  0.63 us (4%)
    pallas_call x1, Pallas kernels, run(): pl.pallas_call(functools.partial(kernel, blks, owners), out_shape=jax.Sha...  14.4 us
    unnamed x1, local copies, waits for them, and re-layouts  0.63 us

profile of v4, /device:TPU:0, one launch (start us, length us, event | category | flops | bytes accessed | tf_op | source)
XLA Modules:
  0.0 15.7 jit_solution(4951635445325776550)
XLA Ops:
  0.7 14.4 %shard_map.100 = bf16[32,1024]{1,0:T(8,128)(2,1)S(1)} custom-call(bf16[32,1024]{1,0:T(8,128)(2,1)} %query_hbm.1, bf16[32,1024]{1,0:T(8,128)(2,1)} %key_hbm.1, bf16[32,1024]{1,0:T(8,128)(2,1)} %value_hbm.1, f32[1,1024]{1,0:T(1,128)} %bitcast.2, f32[1,1024]{1,0:T(1,128)} %bitcast.3, bf16[32,384]{1,0:T(8,128)(2,1)} %control_hbm.1, ...), custom_call_target="tpu_custom_call" | custom-call | tf_op jit(solution)/shard_map/pallas_call | solution.py:499
  15.0 0.6 %copy.13 = bf16[32,1024]{1,0:T(8,128)(2,1)} copy(bf16[32,1024]{1,0:T(8,128)(2,1)S(1)} %shard_map.100) | data formatting | bytes 131072

commit v5 on v4

--- a/solution.py
+++ b/solution.py
@@ -189,6 +189,8 @@
     first_plane = u == 0
     last_plane = u == owners - 1
     leading = u == low
+    last_core = lax.rem(b, CORES) == CORES - 1
+    relaying = leading & last_core
     near_low = 2 * u < owners
     near = jnp.where(near_low, low, high - 1)
     far = jnp.where(near_low, high - 1, low)
@@ -216,6 +218,10 @@
     @pl.when(first_plane)
     def _():
         signal(barrier, {"ulysses": low})
+
+        @pl.when(jnp.logical_not(last_core))
+        def _():
+            signal(barrier, {"blk": x * CORES + CORES - 1, "ulysses": low})
 
     loads = [
         pltpu.make_async_copy(source, target, load_sem.at[at])
@@ -278,6 +284,9 @@
         value_sem,
     )
 
+    expected = heads - hosting.astype(jnp.int32) + leading.astype(jnp.int32)
+    expected = expected + (CORES - 1) * relaying.astype(jnp.int32)
+
     @pl.when(hosting)
     def _():
         own_values.start()
@@ -290,11 +299,15 @@
 
     @pl.when(jnp.logical_not(first_plane))
     def _():
-        pl.semaphore_wait(barrier, heads - hosting.astype(jnp.int32) + leading.astype(jnp.int32))
+        pl.semaphore_wait(barrier, expected)
+
+        @pl.when(relaying)
+        def _():
+            for core in range(CORES):
+                signal(far_sem, {"blk": x * CORES + core, "ulysses": 0})
 
         @pl.when(leading)
         def _():
-            signal(far_sem, {"ulysses": 0})
             signal(line_sem, {"ulysses": far})
 
         @pl.when(last_plane)

time: 15.8 us -> 15.7 us (level)
  no operation moved by 1% of the time
where the time goes in v5:
time: 15.7 us; the launch traced here: 15.5 us
  Pallas kernels  14.3 us (91%)
  between operations  0.66 us (4%)
  local copies, waits for them, and re-layouts  0.63 us (4%)
    pallas_call x1, Pallas kernels, run(): pl.pallas_call(functools.partial(kernel, blks, owners), out_shape=jax.Sha...  14.3 us
    unnamed x1, local copies, waits for them, and re-layouts  0.63 us

profile of v5, /device:TPU:0, one launch (start us, length us, event | category | flops | bytes accessed | tf_op | source)
XLA Modules:
  0.0 15.5 jit_solution(10884549662661018009)
XLA Ops:
  0.7 14.3 %shard_map.100 = bf16[32,1024]{1,0:T(8,128)(2,1)S(1)} custom-call(bf16[32,1024]{1,0:T(8,128)(2,1)} %query_hbm.1, bf16[32,1024]{1,0:T(8,128)(2,1)} %key_hbm.1, bf16[32,1024]{1,0:T(8,128)(2,1)} %value_hbm.1, f32[1,1024]{1,0:T(1,128)} %bitcast.2, f32[1,1024]{1,0:T(1,128)} %bitcast.3, bf16[32,384]{1,0:T(8,128)(2,1)} %control_hbm.1, ...), custom_call_target="tpu_custom_call" | custom-call | tf_op jit(solution)/shard_map/pallas_call | solution.py:512
  14.9 0.6 %copy.13 = bf16[32,1024]{1,0:T(8,128)(2,1)} copy(bf16[32,1024]{1,0:T(8,128)(2,1)S(1)} %shard_map.100) | data formatting | bytes 131072

commit v6 on v5

--- a/solution.py
+++ b/solution.py
@@ -202,7 +202,7 @@
     barrier = pltpu.get_barrier_semaphore()
     @pl.when(hosting)
     def _():
-        for to_b in range(blks):
+        for to_b in sorted(range(blks), key=lambda at: -(at % CORES)):
             signal(barrier, {"blk": to_b, "ulysses": far})
 
         @pl.when(leading)
@@ -493,6 +493,7 @@
         and heads * HEAD_DIM == feats
         and (low, high) == (1, owners - 1)
         and high - low == 2
+        and blks == 2 * CORES
         and rows % 16 == 0
         and rows % owners == 0
         and (rows // owners) % 8 == 0

time: 15.7 us -> 15.7 us (level)
  no operation moved by 1% of the time
where the time goes in v6:
time: 15.7 us; the launch traced here: 15.6 us
  Pallas kernels  14.3 us (91%)
  between operations  0.66 us (4%)
  local copies, waits for them, and re-layouts  0.63 us (4%)
    pallas_call x1, Pallas kernels, run(): pl.pallas_call(functools.partial(kernel, blks, owners), out_shape=jax.Sha...  14.3 us
    unnamed x1, local copies, waits for them, and re-layouts  0.63 us

profile of v6, /device:TPU:0, one launch (start us, length us, event | category | flops | bytes accessed | tf_op | source)
XLA Modules:
  0.0 15.6 jit_solution(10000049815343916485)
XLA Ops:
  0.7 14.3 %shard_map.100 = bf16[32,1024]{1,0:T(8,128)(2,1)S(1)} custom-call(bf16[32,1024]{1,0:T(8,128)(2,1)} %query_hbm.1, bf16[32,1024]{1,0:T(8,128)(2,1)} %key_hbm.1, bf16[32,1024]{1,0:T(8,128)(2,1)} %value_hbm.1, f32[1,1024]{1,0:T(1,128)} %bitcast.2, f32[1,1024]{1,0:T(1,128)} %bitcast.3, bf16[32,384]{1,0:T(8,128)(2,1)} %control_hbm.1, ...), custom_call_target="tpu_custom_call" | custom-call | tf_op jit(solution)/shard_map/pallas_call | solution.py:513
  14.9 0.6 %copy.13 = bf16[32,1024]{1,0:T(8,128)(2,1)} copy(bf16[32,1024]{1,0:T(8,128)(2,1)S(1)} %shard_map.100) | data formatting | bytes 131072
